TPU v7x, 512 devices: a whole 4x4x16 slice. The times are simulated.
512 devices in a mesh: guide: 2 (over core), patch: 256 (over x, y, z).
Axes of the slice: x: 4, y: 4, z: 16, core: 2. Of those that a mesh axis runs over, the one named last changes fastest.
Arguments:
- queries: bfloat16 [2, 28672, 128], P('guide', 'patch'), may hold values from -40 to 40
- fresh_keys: bfloat16 [2, 28672, 128], P('guide', 'patch'), may hold values from -9.5625 to 9.5625
- fresh_values: bfloat16 [2, 28672, 128], P('guide', 'patch'), may hold values from -6 to 6
- stale_keys: bfloat16 [2, 28672, 128], P('guide', 'patch'), may hold values from -10 to 10
- stale_values: bfloat16 [2, 28672, 128], P('guide', 'patch'), may hold values from -6 to 6
- hidden: bfloat16 [2, 28672, 5120], P('guide', 'patch'), may hold values from -6 to 6
- out_weight: bfloat16 [128, 5120], replicated, may hold values from -0.5 to 0.5
- modulation: float32 [5120], replicated, may hold values from 1 to 4
Outputs:
- guided: bfloat16 [28672, 5120], P('patch', 'guide')
All inputs are finite; a program needn't handle non-finite values.
Results may differ from a plain program's by a relative error of at most 0.0051.
Values may be sent and summed in bfloat16 or wider, within the bound.
No kernel may reach another device: no remote copies, remote signals or barrier semaphores. Data moves between devices by JAX's collectives and lax.ppermute only.
A program may use at most 64 MiB of HBM per device.

v0:
```python
import math
import jax
import jax.numpy as jnp
from jax import lax
from jax.sharding import PartitionSpec as P

GUIDANCE = 5.0


def swapped(value, axis, stride):
    mask = 2**stride
    pairs = [(source, source ^ mask) for source in range(lax.axis_size(axis))]
    return lax.ppermute(value, axis, pairs)


def block_length(local_rows, patches):
    shards = 1
    while shards * 2 * local_rows <= 4096 and patches % (shards * 2) == 0:
        shards = shards * 2
    return shards * local_rows


def on_device(
    queries, fresh_keys, fresh_values, stale_keys, stale_values, hidden, out_weight, modulation
):
    query_rows = queries[0]
    keys_fresh = fresh_keys[0]
    values_fresh = fresh_values[0]
    local_rows = query_rows.shape[0]
    head_width = query_rows.shape[1]
    patches = lax.axis_size("patch")
    own_start = lax.axis_index("patch") * local_rows
    score_scale = 1.0 / math.sqrt(head_width)
    block_size = block_length(local_rows, patches)

    def refresh(piece_keys, piece_values, first_row):
        piece_rows = piece_keys.shape[0]
        position = first_row + jnp.arange(piece_rows, dtype=jnp.int32)
        inside = (position >= own_start) & (position < own_start + local_rows)
        offset = jnp.clip(position - own_start, 0, local_rows - 1)
        new_keys = jnp.where(inside[:, None], jnp.take(keys_fresh, offset, axis=0), piece_keys)
        new_values = jnp.where(
            inside[:, None], jnp.take(values_fresh, offset, axis=0), piece_values
        )
        return (new_keys, new_values)

    def attend_block(running, piece_keys, piece_values, first_row):
        running_max, running_sum, running_acc = running
        piece_keys, piece_values = refresh(piece_keys, piece_values, first_row)
        scores = (
            lax.dot_general(
                query_rows, piece_keys, (((1,), (1,)), ((), ())), preferred_element_type=jnp.float32
            )
            * score_scale
        )
        new_max = jnp.maximum(running_max, jnp.max(scores, axis=1))
        factor = jnp.exp(running_max - new_max)
        weights = jnp.exp(scores - new_max[:, None]).astype(jnp.bfloat16)
        new_sum = running_sum * factor + jnp.sum(weights.astype(jnp.float32), axis=1)
        new_acc = running_acc * factor[:, None] + jnp.dot(
            weights, piece_values, preferred_element_type=jnp.float32
        )
        return (new_max, new_sum, new_acc)

    initial = (
        jnp.full((local_rows,), -1e30, jnp.float32),
        jnp.zeros((local_rows,), jnp.float32),
        jnp.zeros((local_rows, head_width), jnp.float32),
    )
    all_keys, all_values = (
        lax.all_gather(stale_keys[0], "patch", axis=0, tiled=True),
        lax.all_gather(stale_values[0], "patch", axis=0, tiled=True),
    )
    running = initial
    piece_keys = all_keys
    piece_values = all_values
    piece_rows = piece_keys.shape[0]
    step_rows = math.gcd(piece_rows, block_size)
    step_count = piece_rows // step_rows
    grouped_keys = piece_keys.reshape(step_count, step_rows, head_width)
    grouped_values = piece_values.reshape(step_count, step_rows, head_width)

    def advance(current, element):
        number, block_keys, block_values = element
        return (attend_block(current, block_keys, block_values, number * step_rows), None)

    running, unused = lax.scan(
        advance, running, (jnp.arange(step_count, dtype=jnp.int32), grouped_keys, grouped_values)
    )
    attention = (running[2] / running[1][:, None]).astype(jnp.bfloat16)
    projected = jnp.dot(attention, out_weight, preferred_element_type=jnp.float32)
    branch_out = (hidden[0].astype(jnp.float32) + modulation[None, :] * projected).astype(
        jnp.bfloat16
    )
    half_width = branch_out.shape[1] // 2
    side = lax.axis_index("guide")
    partner = swapped(branch_out, "guide", 0)
    conditional = jnp.where(side == 0, branch_out, partner)
    unconditional = jnp.where(side == 0, partner, branch_out)
    conditional = lax.dynamic_slice_in_dim(conditional, side * half_width, half_width, 1)
    unconditional = lax.dynamic_slice_in_dim(unconditional, side * half_width, half_width, 1)
    cond_value = conditional.astype(jnp.float32)
    uncond_value = unconditional.astype(jnp.float32)
    return (uncond_value + GUIDANCE * (cond_value - uncond_value)).astype(jnp.bfloat16)


def solution(mesh):
    in_specs = (
        P("guide", "patch", None),
        P("guide", "patch", None),
        P("guide", "patch", None),
        P("guide", "patch", None),
        P("guide", "patch", None),
        P("guide", "patch", None),
        P(),
        P(),
    )
    out_specs = P("patch", "guide")
    return jax.shard_map(
        on_device, mesh=mesh, in_specs=in_specs, out_specs=out_specs, check_vma=False
    )
```

profile of v0, /device:TPU:1, one launch (start us, length us, event | category | flops | bytes accessed | tf_op | source)
XLA Modules:
  0.0 678.7 jit_solution(15807300499211732269)
XLA Ops:
  6.5 0.7 all-gather.5.cloned.1.call-update
  7.3 0.7 all-gather.7.cloned.1.call-update
  8.0 217.2 %all-gather.5.cloned.1.call-done = bf16[1,28672,128]{2,1,0:T(8,128)(2,1)} async-done(((bf16[1,112,128]{2,1,0:T(8,128)(2,1)}), bf16[1,28672,128]{2,1,0:T(8,128)(2,1)}) %all-gather.5.cloned.1.call-update) | async-done | bytes 7340048 | tf_op jit(solution)/shard_map/all_gather | solution.py:71
  225.3 216.4 %all-gather.7.cloned.1.call-done = bf16[1,28672,128]{2,1,0:T(8,128)(2,1)} async-done(((bf16[1,112,128]{2,1,0:T(8,128)(2,1)}), bf16[1,28672,128]{2,1,0:T(8,128)(2,1)}) %all-gather.7.cloned.1.call-update) | async-done | bytes 7340048 | tf_op jit(solution)/shard_map/all_gather | solution.py:72
  441.6 212.1 %while.16 = (s32[]{:T(128)}, f32[112]{0:T(128)S(1)}, f32[112]{0:T(128)S(1)}, f32[112,128]{1,0:T(8,128)S(1)}, s32[8]{0:T(128)S(1)}, /*index=5*/s32[]{:T(128)}, s3...) while((s32[]{:T(128)}, f32[112]{0:T(128)S(1)}, ...), condition=%wide.region_3.5_spmd.clone, body=%wide.region_0.4_spmd.clone.sunk | while | flops 210679344 | bytes 12748057 | solution.py:87
  441.6 0.6 dynamic_slice.46
  442.9 8.1 %gather_fusion = bf16[3584,128]{1,0:T(8,128)(2,1)} fusion(bf16[112,128]{1,0:T(8,128)(2,1)S(1)} %copy-done.1, s32[4096]{0:T(1024)S(1)} %pad_clamp_fusion.2), kind=kCustom, calls=%fused_computation.clone.clone.1 | custom fusion | bytes 1849344 | tf_op jit(solution)/shard_map/while/body/eval_jaxpr/jit(_take)/gather | solution.py:41
  451.0 4.5 fusion.35
  455.5 0.4 convert_reduce_fusion.2
  455.9 0.3 copy-done.2
  456.2 8.1 %gather_fusion.1 = bf16[3584,128]{1,0:T(8,128)(2,1)} fusion(bf16[112,128]{1,0:T(8,128)(2,1)S(1)} %copy-done.2, s32[4096]{0:T(1024)S(1)} %pad_clamp_fusion.2), kind=kCustom, calls=%fused_computation.1.clone.clone.1 | custom fusion | bytes 1849344 | tf_op jit(solution)/shard_map/while/body/eval_jaxpr/jit(_take)/gather | solution.py:43
  464.4 3.8 convolution_add_fusion.2
  468.2 0.6 dynamic_slice.46
  469.4 8.1 %gather_fusion = bf16[3584,128]{1,0:T(8,128)(2,1)} fusion(bf16[112,128]{1,0:T(8,128)(2,1)S(1)} %copy-done.1, s32[4096]{0:T(1024)S(1)} %pad_clamp_fusion.2), kind=kCustom, calls=%fused_computation.clone.clone.1 | custom fusion | bytes 1849344 | tf_op jit(solution)/shard_map/while/body/eval_jaxpr/jit(_take)/gather | solution.py:41
  477.5 4.5 fusion.35
  482.0 0.4 convert_reduce_fusion.2
  482.4 0.3 copy-done.2
  482.7 8.1 %gather_fusion.1 = bf16[3584,128]{1,0:T(8,128)(2,1)} fusion(bf16[112,128]{1,0:T(8,128)(2,1)S(1)} %copy-done.2, s32[4096]{0:T(1024)S(1)} %pad_clamp_fusion.2), kind=kCustom, calls=%fused_computation.1.clone.clone.1 | custom fusion | bytes 1849344 | tf_op jit(solution)/shard_map/while/body/eval_jaxpr/jit(_take)/gather | solution.py:43
  490.9 3.8 convolution_add_fusion.2
  494.7 0.6 dynamic_slice.46
  495.9 8.1 %gather_fusion = bf16[3584,128]{1,0:T(8,128)(2,1)} fusion(bf16[112,128]{1,0:T(8,128)(2,1)S(1)} %copy-done.1, s32[4096]{0:T(1024)S(1)} %pad_clamp_fusion.2), kind=kCustom, calls=%fused_computation.clone.clone.1 | custom fusion | bytes 1849344 | tf_op jit(solution)/shard_map/while/body/eval_jaxpr/jit(_take)/gather | solution.py:41
  504.0 4.5 fusion.35
  508.5 0.4 convert_reduce_fusion.2
  508.9 0.3 copy-done.2
  509.3 8.1 %gather_fusion.1 = bf16[3584,128]{1,0:T(8,128)(2,1)} fusion(bf16[112,128]{1,0:T(8,128)(2,1)S(1)} %copy-done.2, s32[4096]{0:T(1024)S(1)} %pad_clamp_fusion.2), kind=kCustom, calls=%fused_computation.1.clone.clone.1 | custom fusion | bytes 1849344 | tf_op jit(solution)/shard_map/while/body/eval_jaxpr/jit(_take)/gather | solution.py:43
  517.4 3.8 convolution_add_fusion.2
  521.2 0.6 dynamic_slice.46
  522.4 8.1 %gather_fusion = bf16[3584,128]{1,0:T(8,128)(2,1)} fusion(bf16[112,128]{1,0:T(8,128)(2,1)S(1)} %copy-done.1, s32[4096]{0:T(1024)S(1)} %pad_clamp_fusion.2), kind=kCustom, calls=%fused_computation.clone.clone.1 | custom fusion | bytes 1849344 | tf_op jit(solution)/shard_map/while/body/eval_jaxpr/jit(_take)/gather | solution.py:41
  530.6 4.5 fusion.35
  535.0 0.4 convert_reduce_fusion.2
  535.4 0.3 copy-done.2
  535.8 8.1 %gather_fusion.1 = bf16[3584,128]{1,0:T(8,128)(2,1)} fusion(bf16[112,128]{1,0:T(8,128)(2,1)S(1)} %copy-done.2, s32[4096]{0:T(1024)S(1)} %pad_clamp_fusion.2), kind=kCustom, calls=%fused_computation.1.clone.clone.1 | custom fusion | bytes 1849344 | tf_op jit(solution)/shard_map/while/body/eval_jaxpr/jit(_take)/gather | solution.py:43
  543.9 3.8 convolution_add_fusion.2
  547.7 0.6 dynamic_slice.46
  548.9 8.1 %gather_fusion = bf16[3584,128]{1,0:T(8,128)(2,1)} fusion(bf16[112,128]{1,0:T(8,128)(2,1)S(1)} %copy-done.1, s32[4096]{0:T(1024)S(1)} %pad_clamp_fusion.2), kind=kCustom, calls=%fused_computation.clone.clone.1 | custom fusion | bytes 1849344 | tf_op jit(solution)/shard_map/while/body/eval_jaxpr/jit(_take)/gather | solution.py:41
  557.1 4.5 fusion.35
  561.6 0.4 convert_reduce_fusion.2
  562.0 0.3 copy-done.2
  562.3 8.1 %gather_fusion.1 = bf16[3584,128]{1,0:T(8,128)(2,1)} fusion(bf16[112,128]{1,0:T(8,128)(2,1)S(1)} %copy-done.2, s32[4096]{0:T(1024)S(1)} %pad_clamp_fusion.2), kind=kCustom, calls=%fused_computation.1.clone.clone.1 | custom fusion | bytes 1849344 | tf_op jit(solution)/shard_map/while/body/eval_jaxpr/jit(_take)/gather | solution.py:43
  570.4 3.8 convolution_add_fusion.2
  574.2 0.6 dynamic_slice.46
  575.5 8.1 %gather_fusion = bf16[3584,128]{1,0:T(8,128)(2,1)} fusion(bf16[112,128]{1,0:T(8,128)(2,1)S(1)} %copy-done.1, s32[4096]{0:T(1024)S(1)} %pad_clamp_fusion.2), kind=kCustom, calls=%fused_computation.clone.clone.1 | custom fusion | bytes 1849344 | tf_op jit(solution)/shard_map/while/body/eval_jaxpr/jit(_take)/gather | solution.py:41
  583.6 4.5 fusion.35
  588.1 0.4 convert_reduce_fusion.2
  588.5 0.3 copy-done.2
  588.8 8.1 %gather_fusion.1 = bf16[3584,128]{1,0:T(8,128)(2,1)} fusion(bf16[112,128]{1,0:T(8,128)(2,1)S(1)} %copy-done.2, s32[4096]{0:T(1024)S(1)} %pad_clamp_fusion.2), kind=kCustom, calls=%fused_computation.1.clone.clone.1 | custom fusion | bytes 1849344 | tf_op jit(solution)/shard_map/while/body/eval_jaxpr/jit(_take)/gather | solution.py:43
  596.9 3.8 convolution_add_fusion.2
  600.7 0.6 dynamic_slice.46
  602.0 8.1 %gather_fusion = bf16[3584,128]{1,0:T(8,128)(2,1)} fusion(bf16[112,128]{1,0:T(8,128)(2,1)S(1)} %copy-done.1, s32[4096]{0:T(1024)S(1)} %pad_clamp_fusion.2), kind=kCustom, calls=%fused_computation.clone.clone.1 | custom fusion | bytes 1849344 | tf_op jit(solution)/shard_map/while/body/eval_jaxpr/jit(_take)/gather | solution.py:41
  610.1 4.5 fusion.35
  614.6 0.4 convert_reduce_fusion.2
  615.0 0.3 copy-done.2
  615.3 8.1 %gather_fusion.1 = bf16[3584,128]{1,0:T(8,128)(2,1)} fusion(bf16[112,128]{1,0:T(8,128)(2,1)S(1)} %copy-done.2, s32[4096]{0:T(1024)S(1)} %pad_clamp_fusion.2), kind=kCustom, calls=%fused_computation.1.clone.clone.1 | custom fusion | bytes 1849344 | tf_op jit(solution)/shard_map/while/body/eval_jaxpr/jit(_take)/gather | solution.py:43
  623.5 3.8 convolution_add_fusion.2
  627.3 0.6 dynamic_slice.46
  628.5 8.1 %gather_fusion = bf16[3584,128]{1,0:T(8,128)(2,1)} fusion(bf16[112,128]{1,0:T(8,128)(2,1)S(1)} %copy-done.1, s32[4096]{0:T(1024)S(1)} %pad_clamp_fusion.2), kind=kCustom, calls=%fused_computation.clone.clone.1 | custom fusion | bytes 1849344 | tf_op jit(solution)/shard_map/while/body/eval_jaxpr/jit(_take)/gather | solution.py:41
  636.6 4.5 fusion.35
  641.1 0.4 convert_reduce_fusion.2
  641.8 8.1 %gather_fusion.1 = bf16[3584,128]{1,0:T(8,128)(2,1)} fusion(bf16[112,128]{1,0:T(8,128)(2,1)S(1)} %copy-done.2, s32[4096]{0:T(1024)S(1)} %pad_clamp_fusion.2), kind=kCustom, calls=%fused_computation.1.clone.clone.1 | custom fusion | bytes 1849344 | tf_op jit(solution)/shard_map/while/body/eval_jaxpr/jit(_take)/gather | solution.py:43
  650.0 3.8 convolution_add_fusion.2
  653.8 1.8 fusion.21
  655.6 11.6 %collective-permute-start = (bf16[112,5120]{1,0:T(8,128)(2,1)S(1)}, bf16[112,5120]{1,0:T(8,128)(2,1)}, u32[]{:S(2)}, u32[]{:S(2)}) collective-permute-start(bf16[112,5120]{1,0:T(8,128)(2,1)S(1)} %fusion.21), channel_id=1, source_target_pairs={{0,256},{256,0},{1,257},{257,1},{2,258},{258,2},{3,259},{259,3},{4... | collective-permute-start | bytes 3440648 | tf_op jit(solution)/shard_map/ppermute | solution.py:13
  667.1 2.5 collective-permute-done
  669.7 2.1 fusion.23
  (99 shorter events, 1.1 us)
Async XLA Ops:
  6.5 647.2 %copy-start = (bf16[128,5120]{1,0:T(8,128)(2,1)S(1)}, bf16[128,5120]{1,0:T(8,128)(2,1)}, u32[]{:S(2)}) copy-start(bf16[128,5120]{1,0:T(8,128)(2,1)} %param.18) | copy-start | bytes 3932164
  6.5 218.7 %all-gather.5.cloned.1.call-start = ((), (), s32[]{:S(2)}) async-start(), calls=%async_computation | async-start | bytes 7368704 | tf_op jit(solution)/shard_map/all_gather | solution.py:71
  7.3 434.4 %all-gather.7.cloned.1.call-start = ((), (), s32[]{:S(2)}) async-start(), calls=%async_computation.1 | async-start | bytes 7368704 | tf_op jit(solution)/shard_map/all_gather | solution.py:72
  441.6 212.1 %copy-start.3 = (f32[5120]{0:T(1024)S(1)}, f32[5120]{0:T(1024)}, u32[]{:S(2)}) copy-start(f32[5120]{0:T(1024)} %param.19) | copy-start | bytes 61444
  441.6 1.2 copy-start.1
  442.9 8.2 %copy-start.4 = (bf16[112,128]{1,0:T(8,128)(2,1)S(1)}, bf16[112,128]{1,0:T(8,128)(2,1)}, u32[]{:S(2)}) copy-start(bf16[112,128]{1,0:T(8,128)(2,1)} %get-tuple-element.308) | copy-start | bytes 86020 | tf_op jit(solution)/shard_map/while
  455.5 0.8 copy-start.2
  468.1 1.2 copy-start.1
  469.4 8.2 %copy-start.4 = (bf16[112,128]{1,0:T(8,128)(2,1)S(1)}, bf16[112,128]{1,0:T(8,128)(2,1)}, u32[]{:S(2)}) copy-start(bf16[112,128]{1,0:T(8,128)(2,1)} %get-tuple-element.308) | copy-start | bytes 86020 | tf_op jit(solution)/shard_map/while
  482.0 0.8 copy-start.2
  494.7 1.2 copy-start.1
  495.9 8.2 %copy-start.4 = (bf16[112,128]{1,0:T(8,128)(2,1)S(1)}, bf16[112,128]{1,0:T(8,128)(2,1)}, u32[]{:S(2)}) copy-start(bf16[112,128]{1,0:T(8,128)(2,1)} %get-tuple-element.308) | copy-start | bytes 86020 | tf_op jit(solution)/shard_map/while
  508.5 0.8 copy-start.2
  521.2 1.2 copy-start.1
  522.4 8.2 %copy-start.4 = (bf16[112,128]{1,0:T(8,128)(2,1)S(1)}, bf16[112,128]{1,0:T(8,128)(2,1)}, u32[]{:S(2)}) copy-start(bf16[112,128]{1,0:T(8,128)(2,1)} %get-tuple-element.308) | copy-start | bytes 86020 | tf_op jit(solution)/shard_map/while
  535.0 0.8 copy-start.2
  547.7 1.2 copy-start.1
  548.9 8.2 %copy-start.4 = (bf16[112,128]{1,0:T(8,128)(2,1)S(1)}, bf16[112,128]{1,0:T(8,128)(2,1)}, u32[]{:S(2)}) copy-start(bf16[112,128]{1,0:T(8,128)(2,1)} %get-tuple-element.308) | copy-start | bytes 86020 | tf_op jit(solution)/shard_map/while
  561.5 0.8 copy-start.2
  574.2 1.2 copy-start.1
  575.4 8.2 %copy-start.4 = (bf16[112,128]{1,0:T(8,128)(2,1)S(1)}, bf16[112,128]{1,0:T(8,128)(2,1)}, u32[]{:S(2)}) copy-start(bf16[112,128]{1,0:T(8,128)(2,1)} %get-tuple-element.308) | copy-start | bytes 86020 | tf_op jit(solution)/shard_map/while
  588.1 0.8 copy-start.2
  600.7 1.2 copy-start.1
  602.0 8.2 %copy-start.4 = (bf16[112,128]{1,0:T(8,128)(2,1)S(1)}, bf16[112,128]{1,0:T(8,128)(2,1)}, u32[]{:S(2)}) copy-start(bf16[112,128]{1,0:T(8,128)(2,1)} %get-tuple-element.308) | copy-start | bytes 86020 | tf_op jit(solution)/shard_map/while
  614.6 0.8 copy-start.2
  627.2 1.2 copy-start.1
  628.5 8.2 %copy-start.4 = (bf16[112,128]{1,0:T(8,128)(2,1)S(1)}, bf16[112,128]{1,0:T(8,128)(2,1)}, u32[]{:S(2)}) copy-start(bf16[112,128]{1,0:T(8,128)(2,1)} %get-tuple-element.308) | copy-start | bytes 86020 | tf_op jit(solution)/shard_map/while
  641.1 0.8 copy-start.2
  655.6 14.1 %collective-permute-start = (bf16[112,5120]{1,0:T(8,128)(2,1)S(1)}, bf16[112,5120]{1,0:T(8,128)(2,1)}, u32[]{:S(2)}, u32[]{:S(2)}) collective-permute-start(bf16[112,5120]{1,0:T(8,128)(2,1)S(1)} %fusion.21), channel_id=1, source_target_pairs={{0,256},{256,0},{1,257},{257,1},{2,258},{258,2},{3,259},{259,3},{4... | collective-permute-start | bytes 3440648 | tf_op jit(solution)/shard_map/ppermute | solution.py:13
Sparse Core Ops, SparseCore 0:
  11.7 213.5 all-gather.4
  229.6 211.9 all-gather.6
where the time goes:
time: 680 us; the launch traced here: 679 us
  waiting for transfers between devices  438 us (64%)
  local copies, waits for them, and re-layouts  138 us (20%)
  matrix products  67.4 us (10%)
  between operations  13.5 us (2%)
  starting transfers between devices  11.6 us (2%)
    all_gather x1, waiting for transfers between devices, on_device(): lax.all_gather(stale_keys[0], 'patch', axis=0, tiled=True)  217 us
    all_gather x1, waiting for transfers between devices, on_device(): lax.all_gather(stale_values[0], 'patch', axis=0, tiled=True)  216 us
    gather x8, local copies, waits for them, and re-layouts, refresh(): jnp.take(keys_fresh, offset, axis=0)  65.1 us
    gather x8, local copies, waits for them, and re-layouts, refresh(): jnp.take(values_fresh, offset, axis=0)  65 us
    dot_general x8, matrix products, attend_block(): lax.dot_general(query_rows, piece_keys, (((1,), (1,)), ((), ())), preferr...  35.6 us
    dot_general x8, matrix products, attend_block(): jnp.dot(weights, piece_values, preferred_element_type=jnp.float32)  30 us
  transfers between devices with their start and end apart: 3, of which 3 were waited for; matrix products, arithmetic and copies ran while one was open for 0% of the time, Pallas kernels for 0%

commit v1 on v0

--- a/solution.py
+++ b/solution.py
@@ -23,6 +23,19 @@
 def on_device(
     queries, fresh_keys, fresh_values, stale_keys, stale_values, hidden, out_weight, modulation
 ):
+
+    def deliver_inputs_now(slab_in, lane_axis):
+        local_part = jnp.concatenate(
+            lax.all_to_all(
+                jnp.stack([slab_in] * lax.psum(1, lane_axis), 0),
+                axis_name=lane_axis,
+                split_axis=0,
+                concat_axis=0,
+            ),
+            0,
+        )
+        return local_part
+
     query_rows = queries[0]
     keys_fresh = fresh_keys[0]
     values_fresh = fresh_values[0]
@@ -69,7 +82,7 @@
     )
     all_keys, all_values = (
         lax.all_gather(stale_keys[0], "patch", axis=0, tiled=True),
-        lax.all_gather(stale_values[0], "patch", axis=0, tiled=True),
+        deliver_inputs_now(stale_values[0], "patch"),
     )
     running = initial
     piece_keys = all_keys

time: 680 us -> 623 us (0.916)
  waiting for transfers between devices: 438 us -> 352 us
  starting transfers between devices: 11.6 us -> 32.7 us
    all_gather x1 -> x0, waiting for transfers between devices: 216 us -> none  [on_device(): lax.all_gather(stale_values[0], 'patch', axis=0, tiled=True)]
    all_gather x1, waiting for transfers between devices: 217 us -> 328 us  [on_device(): lax.all_gather(stale_keys[0], 'patch', axis=0, tiled=True)]
    all_to_all x0 -> x1, starting transfers between devices: none -> 26.4 us  [deliver_inputs_now(): lax.all_to_all(jnp.stack([slab_in] * lax.psum(1, lane_axis), 0), axis_nam...]
    all_to_all x0 -> x1, waiting for transfers between devices: none -> 21.1 us  [deliver_inputs_now(): lax.all_to_all(jnp.stack([slab_in] * lax.psum(1, lane_axis), 0), axis_nam...]
where the time goes in v1:
time: 623 us; the launch traced here: 617 us
  waiting for transfers between devices  352 us (57%)
  local copies, waits for them, and re-layouts  139 us (22%)
  matrix products  67.4 us (11%)
  starting transfers between devices  32.7 us (5%)
  between operations  13.5 us (2%)
    all_gather x1, waiting for transfers between devices, on_device(): lax.all_gather(stale_keys[0], 'patch', axis=0, tiled=True)  328 us
    gather x8, local copies, waits for them, and re-layouts, refresh(): jnp.take(values_fresh, offset, axis=0)  64.7 us
    gather x8, local copies, waits for them, and re-layouts, refresh(): jnp.take(keys_fresh, offset, axis=0)  64.7 us
    dot_general x8, matrix products, attend_block(): lax.dot_general(query_rows, piece_keys, (((1,), (1,)), ((), ())), preferr...  35.6 us
    dot_general x8, matrix products, attend_block(): jnp.dot(weights, piece_values, preferred_element_type=jnp.float32)  30 us
    all_to_all x1, starting transfers between devices, deliver_inputs_now(): lax.all_to_all(jnp.stack([slab_in] * lax.psum(1, lane_axis), 0), axis_nam...  26.4 us
    all_to_all x1, waiting for transfers between devices, deliver_inputs_now(): lax.all_to_all(jnp.stack([slab_in] * lax.psum(1, lane_axis), 0), axis_nam...  21.1 us
  transfers between devices with their start and end apart: 3, of which 3 were waited for; matrix products, arithmetic and copies ran while one was open for 0% of the time, Pallas kernels for 0%

profile of v1, /device:TPU:1, one launch (start us, length us, event | category | flops | bytes accessed | tf_op | source)
XLA Modules:
  0.0 616.8 jit_solution(14523078242265627327)
XLA Ops:
  6.5 0.0 copy-start
  6.5 4.7 stack.3
  11.3 26.4 %all-to-all-start = ((bf16[256,112,128]{2,1,0:T(8,128)(2,1)}), bf16[256,112,128]{2,1,0:T(8,128)(2,1)}, u32[]{:S(2)}, u32[]{:S(2)}) async-start(bf16[256,112,128]{2,1,0:T(8,128)(2,1)} %stack.3), calls=%async_computation | async-start | bytes 14680064 | tf_op jit(solution)/shard_map/all_to_all | solution.py:29
  37.7 0.0 all-gather.3.cloned.1.call-start
  37.7 0.7 all-gather.3.cloned.1.call-update
  38.4 327.7 %all-gather.3.cloned.1.call-done = bf16[1,28672,128]{2,1,0:T(8,128)(2,1)} async-done(((bf16[1,112,128]{2,1,0:T(8,128)(2,1)}), bf16[1,28672,128]{2,1,0:T(8,128)(2,1)}) %all-gather.3.cloned.1.call-update) | async-done | bytes 7340048 | tf_op jit(solution)/shard_map/all_gather | solution.py:84
  366.1 21.1 %all-to-all-done = bf16[256,112,128]{2,1,0:T(8,128)(2,1)} async-done(((bf16[256,112,128]{2,1,0:T(8,128)(2,1)}), bf16[256,112,128]{2,1,0:T(8,128)(2,1)}, u32[]{:S(2)}, u32[]{:S(2)}) %all-to-all-start) | async-done | bytes 7340064 | tf_op jit(solution)/shard_map/all_to_all | solution.py:29
  387.2 0.0 copy-done.1
  387.2 0.0 copy-done.2
  387.2 0.0 copy-done.4
  387.2 0.0 copy-start.3
  387.2 210.0 %while.16 = (s32[]{:T(128)}, f32[112]{0:T(128)S(1)}, f32[112]{0:T(128)S(1)}, f32[112,128]{1,0:T(8,128)S(1)}, s32[8]{0:T(128)S(1)}, /*index=5*/s32[]{:T(128)}, s3...) while((s32[]{:T(128)}, f32[112]{0:T(128)S(1)}, ...), condition=%wide.region_3.5_spmd.clone, body=%wide.region_0.4_spmd.clone.sunk | while | flops 210679344 | bytes 12403909 | solution.py:100
  387.2 0.7 dynamic_slice.46
  388.7 8.1 %gather_fusion = bf16[3584,128]{1,0:T(8,128)(2,1)} fusion(bf16[112,128]{1,0:T(8,128)(2,1)S(1)} %get-tuple-element.306, s32[4096]{0:T(1024)S(1)} %pad_clamp_fusion.2), kind=kCustom, calls=%fused_computation.clone.clone.1 | custom fusion | bytes 1849344 | tf_op jit(solution)/shard_map/while/body/eval_jaxpr/jit(_take)/gather | solution.py:54
  396.8 4.5 fusion.35
  401.2 0.4 convert_reduce_fusion.2
  401.6 8.1 %gather_fusion.1 = bf16[3584,128]{1,0:T(8,128)(2,1)} fusion(bf16[112,128]{1,0:T(8,128)(2,1)S(1)} %get-tuple-element.309, s32[4096]{0:T(1024)S(1)} %pad_clamp_fusion.2), kind=kCustom, calls=%fused_computation.1.clone.clone.1 | custom fusion | bytes 1849344 | tf_op jit(solution)/shard_map/while/body/eval_jaxpr/jit(_take)/gather | solution.py:56
  409.7 3.8 convolution_add_fusion.2
  413.5 0.7 dynamic_slice.46
  414.9 8.1 %gather_fusion = bf16[3584,128]{1,0:T(8,128)(2,1)} fusion(bf16[112,128]{1,0:T(8,128)(2,1)S(1)} %get-tuple-element.306, s32[4096]{0:T(1024)S(1)} %pad_clamp_fusion.2), kind=kCustom, calls=%fused_computation.clone.clone.1 | custom fusion | bytes 1849344 | tf_op jit(solution)/shard_map/while/body/eval_jaxpr/jit(_take)/gather | solution.py:54
  423.0 4.4 fusion.35
  427.5 0.4 convert_reduce_fusion.2
  427.9 8.1 %gather_fusion.1 = bf16[3584,128]{1,0:T(8,128)(2,1)} fusion(bf16[112,128]{1,0:T(8,128)(2,1)S(1)} %get-tuple-element.309, s32[4096]{0:T(1024)S(1)} %pad_clamp_fusion.2), kind=kCustom, calls=%fused_computation.1.clone.clone.1 | custom fusion | bytes 1849344 | tf_op jit(solution)/shard_map/while/body/eval_jaxpr/jit(_take)/gather | solution.py:56
  436.0 3.8 convolution_add_fusion.2
  439.7 0.7 dynamic_slice.46
  441.2 8.1 %gather_fusion = bf16[3584,128]{1,0:T(8,128)(2,1)} fusion(bf16[112,128]{1,0:T(8,128)(2,1)S(1)} %get-tuple-element.306, s32[4096]{0:T(1024)S(1)} %pad_clamp_fusion.2), kind=kCustom, calls=%fused_computation.clone.clone.1 | custom fusion | bytes 1849344 | tf_op jit(solution)/shard_map/while/body/eval_jaxpr/jit(_take)/gather | solution.py:54
  449.3 4.5 fusion.35
  453.7 0.4 convert_reduce_fusion.2
  454.1 8.1 %gather_fusion.1 = bf16[3584,128]{1,0:T(8,128)(2,1)} fusion(bf16[112,128]{1,0:T(8,128)(2,1)S(1)} %get-tuple-element.309, s32[4096]{0:T(1024)S(1)} %pad_clamp_fusion.2), kind=kCustom, calls=%fused_computation.1.clone.clone.1 | custom fusion | bytes 1849344 | tf_op jit(solution)/shard_map/while/body/eval_jaxpr/jit(_take)/gather | solution.py:56
  462.2 3.8 convolution_add_fusion.2
  466.0 0.7 dynamic_slice.46
  467.4 8.1 %gather_fusion = bf16[3584,128]{1,0:T(8,128)(2,1)} fusion(bf16[112,128]{1,0:T(8,128)(2,1)S(1)} %get-tuple-element.306, s32[4096]{0:T(1024)S(1)} %pad_clamp_fusion.2), kind=kCustom, calls=%fused_computation.clone.clone.1 | custom fusion | bytes 1849344 | tf_op jit(solution)/shard_map/while/body/eval_jaxpr/jit(_take)/gather | solution.py:54
  475.5 4.4 fusion.35
  480.0 0.4 convert_reduce_fusion.2
  480.4 8.1 %gather_fusion.1 = bf16[3584,128]{1,0:T(8,128)(2,1)} fusion(bf16[112,128]{1,0:T(8,128)(2,1)S(1)} %get-tuple-element.309, s32[4096]{0:T(1024)S(1)} %pad_clamp_fusion.2), kind=kCustom, calls=%fused_computation.1.clone.clone.1 | custom fusion | bytes 1849344 | tf_op jit(solution)/shard_map/while/body/eval_jaxpr/jit(_take)/gather | solution.py:56
  488.5 3.8 convolution_add_fusion.2
  492.2 0.7 dynamic_slice.46
  493.7 8.1 %gather_fusion = bf16[3584,128]{1,0:T(8,128)(2,1)} fusion(bf16[112,128]{1,0:T(8,128)(2,1)S(1)} %get-tuple-element.306, s32[4096]{0:T(1024)S(1)} %pad_clamp_fusion.2), kind=kCustom, calls=%fused_computation.clone.clone.1 | custom fusion | bytes 1849344 | tf_op jit(solution)/shard_map/while/body/eval_jaxpr/jit(_take)/gather | solution.py:54
  501.8 4.5 fusion.35
  506.2 0.4 convert_reduce_fusion.2
  506.6 8.1 %gather_fusion.1 = bf16[3584,128]{1,0:T(8,128)(2,1)} fusion(bf16[112,128]{1,0:T(8,128)(2,1)S(1)} %get-tuple-element.309, s32[4096]{0:T(1024)S(1)} %pad_clamp_fusion.2), kind=kCustom, calls=%fused_computation.1.clone.clone.1 | custom fusion | bytes 1849344 | tf_op jit(solution)/shard_map/while/body/eval_jaxpr/jit(_take)/gather | solution.py:56
  514.7 3.8 convolution_add_fusion.2
  518.5 0.7 dynamic_slice.46
  519.9 8.1 %gather_fusion = bf16[3584,128]{1,0:T(8,128)(2,1)} fusion(bf16[112,128]{1,0:T(8,128)(2,1)S(1)} %get-tuple-element.306, s32[4096]{0:T(1024)S(1)} %pad_clamp_fusion.2), kind=kCustom, calls=%fused_computation.clone.clone.1 | custom fusion | bytes 1849344 | tf_op jit(solution)/shard_map/while/body/eval_jaxpr/jit(_take)/gather | solution.py:54
  528.0 4.4 fusion.35
  532.5 0.4 convert_reduce_fusion.2
  532.9 8.1 %gather_fusion.1 = bf16[3584,128]{1,0:T(8,128)(2,1)} fusion(bf16[112,128]{1,0:T(8,128)(2,1)S(1)} %get-tuple-element.309, s32[4096]{0:T(1024)S(1)} %pad_clamp_fusion.2), kind=kCustom, calls=%fused_computation.1.clone.clone.1 | custom fusion | bytes 1849344 | tf_op jit(solution)/shard_map/while/body/eval_jaxpr/jit(_take)/gather | solution.py:56
  541.0 3.8 convolution_add_fusion.2
  544.8 0.7 dynamic_slice.46
  546.2 8.1 %gather_fusion = bf16[3584,128]{1,0:T(8,128)(2,1)} fusion(bf16[112,128]{1,0:T(8,128)(2,1)S(1)} %get-tuple-element.306, s32[4096]{0:T(1024)S(1)} %pad_clamp_fusion.2), kind=kCustom, calls=%fused_computation.clone.clone.1 | custom fusion | bytes 1849344 | tf_op jit(solution)/shard_map/while/body/eval_jaxpr/jit(_take)/gather | solution.py:54
  554.3 4.5 fusion.35
  558.7 0.4 convert_reduce_fusion.2
  559.1 8.1 %gather_fusion.1 = bf16[3584,128]{1,0:T(8,128)(2,1)} fusion(bf16[112,128]{1,0:T(8,128)(2,1)S(1)} %get-tuple-element.309, s32[4096]{0:T(1024)S(1)} %pad_clamp_fusion.2), kind=kCustom, calls=%fused_computation.1.clone.clone.1 | custom fusion | bytes 1849344 | tf_op jit(solution)/shard_map/while/body/eval_jaxpr/jit(_take)/gather | solution.py:56
  567.2 3.8 convolution_add_fusion.2
  571.0 0.7 dynamic_slice.46
  572.4 8.1 %gather_fusion = bf16[3584,128]{1,0:T(8,128)(2,1)} fusion(bf16[112,128]{1,0:T(8,128)(2,1)S(1)} %get-tuple-element.306, s32[4096]{0:T(1024)S(1)} %pad_clamp_fusion.2), kind=kCustom, calls=%fused_computation.clone.clone.1 | custom fusion | bytes 1849344 | tf_op jit(solution)/shard_map/while/body/eval_jaxpr/jit(_take)/gather | solution.py:54
  580.5 4.4 fusion.35
  585.0 0.4 convert_reduce_fusion.2
  585.4 8.1 %gather_fusion.1 = bf16[3584,128]{1,0:T(8,128)(2,1)} fusion(bf16[112,128]{1,0:T(8,128)(2,1)S(1)} %get-tuple-element.309, s32[4096]{0:T(1024)S(1)} %pad_clamp_fusion.2), kind=kCustom, calls=%fused_computation.1.clone.clone.1 | custom fusion | bytes 1849344 | tf_op jit(solution)/shard_map/while/body/eval_jaxpr/jit(_take)/gather | solution.py:56
  593.5 3.8 convolution_add_fusion.2
  597.3 1.8 fusion.21
  599.1 6.2 %collective-permute-start = (bf16[112,5120]{1,0:T(8,128)(2,1)S(1)}, bf16[112,5120]{1,0:T(8,128)(2,1)}, u32[]{:S(2)}, u32[]{:S(2)}) collective-permute-start(bf16[112,5120]{1,0:T(8,128)(2,1)S(1)} %fusion.21), channel_id=1, source_target_pairs={{0,256},{256,0},{1,257},{257,1},{2,258},{258,2},{3,259},{259,3},{4... | collective-permute-start | bytes 3440648 | tf_op jit(solution)/shard_map/ppermute | solution.py:13
  605.3 2.5 collective-permute-done
  607.8 2.2 fusion.23
  (57 shorter events, 0.6 us)
Async XLA Ops:
  6.5 590.7 %copy-start = (bf16[128,5120]{1,0:T(8,128)(2,1)S(1)}, bf16[128,5120]{1,0:T(8,128)(2,1)}, u32[]{:S(2)}) copy-start(bf16[128,5120]{1,0:T(8,128)(2,1)} %param.18) | copy-start | bytes 3932164
  11.3 376.0 %copy-start.1 = (bf16[1,112,128]{2,1,0:T(8,128)(2,1)S(1)}, bf16[1,112,128]{2,1,0:T(8,128)(2,1)}, u32[]{:S(2)}) copy-start(bf16[1,112,128]{2,1,0:T(8,128)(2,1)} %param.13) | copy-start | bytes 86020
  11.3 376.0 %copy-start.2 = (bf16[1,112,128]{2,1,0:T(8,128)(2,1)S(1)}, bf16[1,112,128]{2,1,0:T(8,128)(2,1)}, u32[]{:S(2)}) copy-start(bf16[1,112,128]{2,1,0:T(8,128)(2,1)} %param.14) | copy-start | bytes 86020
  11.3 376.0 %copy-start.4 = (bf16[1,112,128]{2,1,0:T(8,128)(2,1)S(1)}, bf16[1,112,128]{2,1,0:T(8,128)(2,1)}, u32[]{:S(2)}) copy-start(bf16[1,112,128]{2,1,0:T(8,128)(2,1)} %param.12) | copy-start | bytes 86020
  11.3 375.9 %all-to-all-start = ((bf16[256,112,128]{2,1,0:T(8,128)(2,1)}), bf16[256,112,128]{2,1,0:T(8,128)(2,1)}, u32[]{:S(2)}, u32[]{:S(2)}) async-start(bf16[256,112,128]{2,1,0:T(8,128)(2,1)} %stack.3), calls=%async_computation | async-start | bytes 14680064 | tf_op jit(solution)/shard_map/all_to_all | solution.py:29
  37.7 328.5 %all-gather.3.cloned.1.call-start = ((), (), s32[]{:S(2)}) async-start(), calls=%async_computation.1 | async-start | bytes 7368704 | tf_op jit(solution)/shard_map/all_gather | solution.py:84
  387.2 210.0 %copy-start.3 = (f32[5120]{0:T(1024)S(1)}, f32[5120]{0:T(1024)}, u32[]{:S(2)}) copy-start(f32[5120]{0:T(1024)} %param.19) | copy-start | bytes 61444
  599.1 8.8 %collective-permute-start = (bf16[112,5120]{1,0:T(8,128)(2,1)S(1)}, bf16[112,5120]{1,0:T(8,128)(2,1)}, u32[]{:S(2)}, u32[]{:S(2)}) collective-permute-start(bf16[112,5120]{1,0:T(8,128)(2,1)S(1)} %fusion.21), channel_id=1, source_target_pairs={{0,256},{256,0},{1,257},{257,1},{2,258},{258,2},{3,259},{259,3},{4... | collective-permute-start | bytes 3440648 | tf_op jit(solution)/shard_map/ppermute | solution.py:13
Sparse Core Ops, SparseCore 0:
  42.8 323.2 all-gather.2
